TPU v7x, 256 devices: a whole 4x4x8 slice. The times are simulated.
256 devices in a mesh: wide: 32 (over z_hi, x, core), narrow: 8 (over z_lo, y).
Axes of the slice: x: 4, y: 4, z: 8 (z_hi: 4, z_lo: 2; z = z_hi * 2 + z_lo), core: 2. Of those that a mesh axis runs over, the one named last changes fastest.
Arguments:
- resid: bfloat16 [1024, 5120], P('wide'), may hold values from -6 to 6
- final_gain: float32 [5120], replicated, may hold values from 0.25 to 1.75
- unembed: bfloat16 [16384, 5120], P('narrow', 'wide'), may hold values from -12 to 12
- labels: int32 [1024, 4], replicated, may hold values from 0 to 16383
- layer_in: bfloat16 [1024, 5120], P('wide'), may hold values from -6 to 6
- gate_value: bfloat16 [1024, 13824], P('wide', 'narrow'), may hold values from -0.29882812 to 2
- down_weight: bfloat16 [13824, 5120], P('narrow', 'wide'), may hold values from -0.078125 to 0.078125
- basis_in: bfloat16 [5120, 5120], P('wide', 'narrow'), may hold values from -0.078125 to 0.078125
- basis_out: bfloat16 [13824, 13824], P('narrow', 'wide'), may hold values from -0.0546875 to 0.0546875
Outputs:
- corrected: float32 [13824, 5120], P('wide', 'narrow')
All inputs are finite; a program needn't handle non-finite values.
Results may differ from a plain program's by a relative error of at most 0.002.
The roundings to bfloat16 on the way count: a program that leaves them out, or rounds other values in their place, can miss the bound.
Values may be sent and summed in bfloat16 or wider, within the bound.
A program may use at most 128 MiB of HBM per device.

v0:
```python
import jax
import jax.numpy as jnp
from jax import lax
from jax.sharding import PartitionSpec as P

SEQ = 256
EXAMPLES = 4
EPSILON = 1e-05


def sent_to_all(value, axis):
    copies = jnp.broadcast_to(value, (lax.axis_size(axis), *value.shape))
    return lax.all_to_all(copies, axis, split_axis=0, concat_axis=0, tiled=True)


def of_everyone(value, axis):
    return sent_to_all(value, axis).sum(axis=0)


def taken_together(value, axis):
    return sent_to_all(value, axis).max(axis=0)


def contract_last(left, right):
    return lax.dot_general(
        left, right, (((1,), (1,)), ((), ())), preferred_element_type=jnp.float32
    )


def per_device(
    resid, final_gain, unembed, labels, layer_in, gate_value, down_weight, basis_in, basis_out
):
    wide_count = lax.axis_size("wide")
    wide_place = lax.axis_index("wide")
    narrow_place = lax.axis_index("narrow")
    local_tokens, width = resid.shape
    all_tokens, samples = labels.shape
    column_part = width // wide_count
    vocab_part = unembed.shape[0]
    hidden_part = down_weight.shape[0]
    grad_rows = local_tokens * samples
    resid_cols, inputs_cols = (
        lax.all_to_all(resid, "wide", split_axis=1, concat_axis=0, tiled=True),
        lax.all_to_all(layer_in, "wide", split_axis=1, concat_axis=0, tiled=True),
    )
    resid_float = resid_cols.astype(jnp.float32)
    gain_cols = lax.dynamic_slice_in_dim(final_gain, wide_place * column_part, column_part, 0)
    square_sums = of_everyone(jnp.sum(resid_float * resid_float, axis=1), "wide")
    inverse = lax.rsqrt(square_sums / width + EPSILON)
    normed = (resid_float * inverse[:, None] * gain_cols).astype(jnp.bfloat16)
    logits = lax.psum_scatter(
        contract_last(normed, unembed), "wide", scatter_dimension=0, tiled=True
    )
    largest = taken_together(jnp.max(logits, axis=1), "narrow")
    scaled = jnp.exp(logits - largest[:, None])
    totals = of_everyone(jnp.sum(scaled, axis=1), "narrow")
    probs = (scaled / totals[:, None]).astype(jnp.bfloat16)
    common = jnp.dot(
        lax.all_gather(probs, "wide", axis=0, tiled=True),
        unembed,
        preferred_element_type=jnp.float32,
    )
    shifted = labels - narrow_place * vocab_part
    inside = ((shifted >= 0) & (shifted < vocab_part)).astype(jnp.float32)
    picked = (
        jnp.take(unembed, jnp.clip(shifted, 0, vocab_part - 1), axis=0).astype(jnp.float32)
        * inside[:, :, None]
    )
    label_part = (common[:, None, :] - picked).reshape(all_tokens * samples, column_part)
    label_grads = lax.psum(label_part, "narrow")
    grads_local = lax.all_to_all(
        label_grads, "wide", split_axis=0, concat_axis=1, tiled=True
    ).reshape(local_tokens, samples, width)
    resid_local = resid.astype(jnp.float32)
    inverse_local = lax.rsqrt(jnp.mean(resid_local * resid_local, axis=1) + EPSILON)
    inner = jnp.sum(final_gain * grads_local * resid_local[:, None, :], axis=2)
    back = (
        inverse_local[:, None, None] * final_gain * grads_local
        - resid_local[:, None, :] * (inverse_local**3)[:, None, None] * inner[:, :, None] / width
    )
    back = back.astype(jnp.bfloat16).reshape(grad_rows, width)
    hidden_grads = contract_last(back, lax.all_gather(down_weight, "wide", axis=1, tiled=True))
    gated = (
        hidden_grads.reshape(local_tokens, samples, hidden_part)
        * gate_value.astype(jnp.float32)[:, None, :]
    )
    gated = gated.astype(jnp.bfloat16).reshape(grad_rows, hidden_part)
    rotated_part = jnp.dot(
        lax.all_gather(gated, "wide", axis=0, tiled=True),
        basis_out,
        preferred_element_type=jnp.float32,
    )
    rotated = lax.psum(rotated_part, "narrow").astype(jnp.bfloat16)
    inputs_part = jnp.dot(inputs_cols, basis_in, preferred_element_type=jnp.float32)
    inputs_rot = lax.psum(inputs_part, "wide").astype(jnp.bfloat16)
    rot_blocks = rotated.reshape(EXAMPLES, SEQ, samples, rotated.shape[1])
    input_blocks = inputs_rot.reshape(EXAMPLES, SEQ, inputs_rot.shape[1])
    blocks = jnp.einsum(
        "etsj,etd->esjd", rot_blocks, input_blocks, preferred_element_type=jnp.float32
    )
    return jnp.mean(blocks * blocks, axis=(0, 1))


def solution(mesh):
    in_specs = (
        P("wide", None),
        P(),
        P("narrow", "wide"),
        P(),
        P("wide", None),
        P("wide", "narrow"),
        P("narrow", "wide"),
        P("wide", "narrow"),
        P("narrow", "wide"),
    )
    out_specs = P("wide", "narrow")
    return jax.shard_map(
        per_device, mesh=mesh, in_specs=in_specs, out_specs=out_specs, check_vma=False
    )
```

profile of v0, /device:TPU:70, one launch (start us, length us, event | category | flops | bytes accessed | tf_op | source)
XLA Modules:
  0.0 968.3 jit_solution(15569779703708332936)
XLA Ops:
  8.6 26.2 %all_to_all.66 = bf16[32,32,160]{2,0,1:T(8,128)(2,1)S(1)} all-to-all(bf16[32,32,160]{2,0,1:T(8,128)(2,1)S(1)} %copy.52), channel_id=1, replica_groups=mesh['wide'=32,'narrow'=8] {'wide'}, dimensions={1} | all-to-all | bytes 655360 | tf_op jit(solution)/shard_map/all_to_all | solution.py:43
  35.8 6.7 all-to-all-start.1
  42.6 6.6 all-to-all-done.1
  49.6 4.5 fusion.13
  54.1 119.5 %reduce-scatter.2.cloned.1.call-done = f32[32,2048]{1,0:T(8,128)} async-done(((f32[1024,2048]{1,0:T(8,128)}), f32[32,2048]{1,0:T(8,128)}) %reduce-scatter.2.cloned.1.call-update) | async-done | bytes 262160 | tf_op jit(solution)/shard_map/reduce_scatter | solution.py:51
  174.7 10.3 %all_to_all.67 = f32[8,1,32]{2,1,0:T(1,128)S(1)} all-to-all(f32[8,1,32]{2,1,0:T(1,128)S(1)} %broadcast_in_dim.41), channel_id=1, replica_groups=mesh['wide'=32,'narrow'=8] {'narrow'}, dimensions={0} | all-to-all | bytes 2048 | tf_op jit(solution)/shard_map/all_to_all | solution.py:13
  186.2 8.5 all_to_all.68
  202.4 16.9 %gather_fusion = bf16[4096,160]{1,0:T(8,128)(2,1)} fusion(bf16[2048,160]{1,0:T(8,128)(2,1)S(1)} %copy.59, s32[4096]{0:T(1024)S(1)} %broadcast_clamp_fusion), kind=kCustom, calls=%fused_computation | custom fusion | bytes 2637824 | tf_op jit(solution)/shard_map/jit(_take)/gather | solution.py:66
  219.4 34.8 %all-gather.4.cloned.1.call-done = bf16[1024,2048]{1,0:T(8,128)(2,1)} async-done(((bf16[32,2048]{1,0:T(8,128)(2,1)}), bf16[1024,2048]{1,0:T(8,128)(2,1)}) %all-gather.4.cloned.1.call-update) | async-done | bytes 4194320 | tf_op jit(solution)/shard_map/all_gather | solution.py:59
  254.2 3.5 fusion.14
  257.6 2.6 sub.32
  260.3 5.3 sub.33
  265.5 7.0 multiply_subtract_fusion
  272.5 5.1 copy.61
  278.2 89.5 %all-reduce.4.cloned.1.call-done = f32[32,128,160]{1,2,0:T(8,128)} async-done(((f32[32,128,160]{1,2,0:T(8,128)}), f32[32,128,160]{1,2,0:T(8,128)}) %all-reduce.4.cloned.1.call-update) | async-done | bytes 2621456 | tf_op jit(solution)/shard_map/psum | solution.py:70
  367.7 9.0 all-to-all-start.4
  377.0 2.1 mul.153
  379.1 5.7 mul.154
  386.8 58.8 %all-to-all-done.4 = f32[32,128,160]{1,2,0:T(8,128)} async-done(((f32[32,128,160]{1,2,0:T(8,128)}), f32[32,128,160]{1,2,0:T(8,128)}, u32[]{:S(2)}, u32[]{:S(2)}) %all-to-all-start.4) | async-done | bytes 2621472 | tf_op jit(solution)/shard_map/all_to_all | solution.py:71
  445.7 5.1 copy.62
  450.8 4.5 multiply_reduce_fusion.1
  455.4 5.8 reshape.127
  461.2 3.5 subtract_convert_fusion
  464.8 70.3 %all-gather.6.cloned.1.call-done = bf16[1728,5120]{0,1:T(8,128)(2,1)} async-done(((bf16[1728,160]{0,1:T(8,128)(2,1)}), bf16[1728,5120]{0,1:T(8,128)(2,1)}) %all-gather.6.cloned.1.call-update) | async-done | bytes 17694736 | tf_op jit(solution)/shard_map/all_gather | solution.py:82
  535.1 9.0 fusion.6
  546.5 36.9 %all_to_all.69 = bf16[32,32,160]{2,0,1:T(8,128)(2,1)S(1)} all-to-all(bf16[32,32,160]{2,0,1:T(8,128)(2,1)S(1)} %copy.66), channel_id=1, replica_groups=mesh['wide'=32,'narrow'=8] {'wide'}, dimensions={1} | all-to-all | bytes 655360 | tf_op jit(solution)/shard_map/all_to_all | solution.py:44
  585.4 192.2 %all-reduce.6 = bf16[1024,640]{1,0:T(8,128)(2,1)S(1)} all-reduce(f32[1024,640]{1,0:T(8,128)} %fusion.16), channel_id=1, replica_groups=mesh['wide'=32,'narrow'=8] {'wide'}, use_global_device_ids=true, to_apply=%region_11.12 | all-reduce | flops 655360 | bytes 3932160 | tf_op jit(solution)/shard_map/psum | solution.py:95
  777.7 11.7 %fusion.15 = f32[4096,432]{0,1:T(8,128)} fusion(bf16[4096,1728]{1,0:T(8,128)(2,1)} %all-gather.8.cloned.1.call-done, bf16[1728,432]{0,1:T(8,128)(2,1)S(1)} %copy-done), kind=kOutput, calls=%fused_computation.31 | convolution fusion | flops 6115295232 | bytes 22726656 | tf_op jit(solution)/shard_map/dot_general | solution.py:88
  789.4 152.2 %all-reduce.5 = bf16[4096,432]{0,1:T(8,128)(2,1)} all-reduce(f32[4096,432]{0,1:T(8,128)} %fusion.15), channel_id=1, replica_groups=mesh['wide'=32,'narrow'=8] {'narrow'}, use_global_device_ids=true, to_apply=%region_10.11 | all-reduce | flops 1769472 | bytes 10616832 | tf_op jit(solution)/shard_map/psum | solution.py:93
  941.7 6.4 copy.65
  948.1 7.0 reshape.129
  955.0 5.6 multiply_reduce_fusion
  (65 shorter events, 21.8 us)
Async XLA Ops:
  6.5 771.1 %copy-start = (bf16[1728,432]{0,1:T(8,128)(2,1)S(1)}, bf16[1728,432]{0,1:T(8,128)(2,1)}, u32[]{:S(2)}) copy-start(bf16[1728,432]{0,1:T(8,128)(2,1)} %param.17) | copy-start | bytes 4478980
  6.5 36.0 %copy-start.6 = (f32[5120]{0:T(1024)S(1)}, f32[5120]{0:T(1024)}, u32[]{:S(2)}) copy-start(f32[5120]{0:T(1024)} %param.10) | copy-start | bytes 61444
  6.5 43.0 %copy-start.2 = (bf16[2048,160]{0,1:T(8,128)(2,1)S(1)}, bf16[2048,160]{0,1:T(8,128)(2,1)}, u32[]{:S(2)}) copy-start(bf16[2048,160]{0,1:T(8,128)(2,1)} %param.11) | copy-start | bytes 1966084
  35.8 13.5 %all-to-all-start.1 = ((f32[32,1,1024]{2,1,0:T(1,128)}), f32[32,1,1024]{2,1,0:T(1,128)S(1)}, u32[]{:S(2)}, u32[]{:S(2)}) async-start(f32[32,1,1024]{2,1,0:T(1,128)} %broadcast_in_dim.40), calls=%async_computation.1 | async-start | bytes 262144 | tf_op jit(solution)/shard_map/all_to_all | solution.py:13
  42.5 131.2 %reduce-scatter.2.cloned.1.call-start = ((), (), s32[]{:S(2)}) async-start(), calls=%async_computation.7 | async-start | bytes 8650752 | tf_op jit(solution)/shard_map/reduce_scatter | solution.py:51
  54.1 143.0 %copy-start.7 = (s32[1024,4]{0,1:T(4,128)S(1)}, s32[1024,4]{0,1:T(4,128)}, u32[]{:S(2)}) copy-start(s32[1024,4]{0,1:T(4,128)} %param.12) | copy-start | bytes 49156
  54.1 200.1 %all-gather.4.cloned.1.call-start = ((), (), s32[]{:S(2)}) async-start(), calls=%async_computation.8 | async-start | bytes 4325376 | tf_op jit(solution)/shard_map/all_gather | solution.py:59
  196.5 171.2 %all-reduce.4.cloned.1.call-start = ((), (), s32[]{:S(2)}) async-start(), calls=%async_computation.9 | async-start | bytes 5242880 | tf_op jit(solution)/shard_map/psum | solution.py:70
  277.7 257.5 %all-gather.6.cloned.1.call-start = ((), (), s32[]{:S(2)}) async-start(), calls=%async_computation.10 | async-start | bytes 18923520 | tf_op jit(solution)/shard_map/all_gather | solution.py:82
  278.2 98.8 %copy-start.1 = (bf16[32,5120]{1,0:T(8,128)(2,1)S(1)}, bf16[32,5120]{1,0:T(8,128)(2,1)}, u32[]{:S(2)}) copy-start(bf16[32,5120]{1,0:T(8,128)(2,1)} %param.9) | copy-start | bytes 983044
  367.7 77.9 %all-to-all-start.4 = ((f32[32,128,160]{1,2,0:T(8,128)}), f32[32,128,160]{1,2,0:T(8,128)}, u32[]{:S(2)}, u32[]{:S(2)}) async-start(f32[32,128,160]{1,2,0:T(8,128)} %all-reduce.4.cloned.1.call-done), calls=%async_computation.5 | async-start | bytes 5242880 | tf_op jit(solution)/shard_map/all_to_all | solution.py:71
  376.7 400.9 %all-gather.8.cloned.1.call-start = ((), (), s32[]{:S(2)}) async-start(), calls=%async_computation.11 | async-start | bytes 15138816 | tf_op jit(solution)/shard_map/all_gather | solution.py:89
  379.1 5.7 copy-start.5
  464.8 80.8 %copy-start.3 = (bf16[32,5120]{1,0:T(8,128)(2,1)S(1)}, bf16[32,5120]{1,0:T(8,128)(2,1)}, u32[]{:S(2)}) copy-start(bf16[32,5120]{1,0:T(8,128)(2,1)} %param.13) | copy-start | bytes 983044
  544.2 39.2 %copy-start.4 = (bf16[160,640]{1,0:T(8,128)(2,1)S(1)}, bf16[160,640]{1,0:T(8,128)(2,1)}, u32[]{:S(2)}) copy-start(bf16[160,640]{1,0:T(8,128)(2,1)} %param.16) | copy-start | bytes 614404
Sparse Core Ops, SparseCore 0:
  54.2 119.3 reduce-scatter.1
  196.6 57.4 all-gather.3
  277.8 89.9 all-reduce.3
  370.1 164.9 all-gather.5
  545.6 118.2 all-gather.7
where the time goes:
time: 970 us; the launch traced here: 968 us
  blocking collectives  426 us (44%)
  waiting for transfers between devices  380 us (39%)
  local copies, waits for them, and re-layouts  73.3 us (8%)
  matrix products  36.3 us (4%)
  other arithmetic  22.6 us (2%)
  starting transfers between devices  16 us (2%)
  between operations  13.4 us (1%)
    psum x1, blocking collectives, per_device(): inputs_rot = lax.psum(inputs_part, 'wide').astype(jnp.bfloat16)  192 us
    psum x1, blocking collectives, per_device(): rotated = lax.psum(rotated_part, 'narrow').astype(jnp.bfloat16)  152 us
    reduce_scatter x1, waiting for transfers between devices, per_device(): lax.psum_scatter(contract_last(normed, unembed), 'wide', scatter_dimensio...  120 us
    psum x1, waiting for transfers between devices, per_device(): label_grads = lax.psum(label_part, 'narrow')  89.5 us
    all_gather x1, waiting for transfers between devices, per_device(): lax.all_gather(down_weight, 'wide', axis=1, tiled=True)  70.3 us
    all_to_all x1, waiting for transfers between devices, per_device(): lax.all_to_all(label_grads, 'wide', split_axis=0, concat_axis=1, tiled=True)  58.8 us
    all_to_all x1, blocking collectives, per_device(): lax.all_to_all(layer_in, 'wide', split_axis=1, concat_axis=0, tiled=True)  36.9 us
    all_gather x1, waiting for transfers between devices, per_device(): lax.all_gather(probs, 'wide', axis=0, tiled=True)  34.8 us
  transfers between devices with their start and end apart: 7, of which 6 were waited for; matrix products, arithmetic and copies ran while one was open for 6% of the time, Pallas kernels for 0%

commit v1 on v0

--- a/solution.py
+++ b/solution.py
@@ -2,6 +2,7 @@
 import jax.numpy as jnp
 from jax import lax
 from jax.sharding import PartitionSpec as P
+from jax.lax import all_to_all, axis_size
 
 SEQ = 256
 EXAMPLES = 4
@@ -79,7 +80,10 @@
         - resid_local[:, None, :] * (inverse_local**3)[:, None, None] * inner[:, :, None] / width
     )
     back = back.astype(jnp.bfloat16).reshape(grad_rows, width)
-    hidden_grads = contract_last(back, lax.all_gather(down_weight, "wide", axis=1, tiled=True))
+    hidden_grads = contract_last(
+        back,
+        jnp.concatenate(all_to_all(jnp.stack(axis_size("wide") * [down_weight]), "wide", 0, 0), 1),
+    )
     gated = (
         hidden_grads.reshape(local_tokens, samples, hidden_part)
         * gate_value.astype(jnp.float32)[:, None, :]

time: 970 us -> 1300 us (1.34)
  waiting for transfers between devices: 380 us -> 608 us
  blocking collectives: 426 us -> 487 us
  local copies, waits for them, and re-layouts: 73.3 us -> 96 us
    all_to_all x1, waiting for transfers between devices: 58.8 us -> 358 us  [per_device(): all_to_all(jnp.stack(axis_size('wide') * [down_weight]), 'wide', 0, 0)]
    all_gather x1 -> x0, waiting for transfers between devices: 70.3 us -> none  [per_device(): lax.all_gather(down_weight, 'wide', axis=1, tiled=True)]
    all_to_all x0 -> x1, blocking collectives: none -> 58.3 us  [per_device(): lax.all_to_all(label_grads, 'wide', split_axis=0, concat_axis=1, tiled=True)]
    all_to_all x1, blocking collectives: 36.9 us -> 18.9 us  [per_device(): lax.all_to_all(layer_in, 'wide', split_axis=1, concat_axis=0, tiled=True)]
    psum x1, blocking collectives: 192 us -> 210 us  [per_device(): inputs_rot = lax.psum(inputs_part, 'wide').astype(jnp.bfloat16)]
  transfers between devices with their start and end apart: 7 -> 6, of which waited for: 6 -> 5; matrix products, arithmetic and copies ran while one was open for 6% -> 5% of each run, Pallas kernels for 0% -> 0%
where the time goes in v1:
time: 1300 us; the launch traced here: 1290 us
  waiting for transfers between devices  608 us (47%)
  blocking collectives  487 us (37%)
  local copies, waits for them, and re-layouts  96 us (7%)
  matrix products  36.4 us (3%)
  starting transfers between devices  25.3 us (2%)
  other arithmetic  22.2 us (2%)
  between operations  13.4 us (1%)
    all_to_all x1, waiting for transfers between devices, per_device(): all_to_all(jnp.stack(axis_size('wide') * [down_weight]), 'wide', 0, 0)  358 us
    psum x1, blocking collectives, per_device(): inputs_rot = lax.psum(inputs_part, 'wide').astype(jnp.bfloat16)  210 us
    psum x1, blocking collectives, per_device(): rotated = lax.psum(rotated_part, 'narrow').astype(jnp.bfloat16)  155 us
    reduce_scatter x1, waiting for transfers between devices, per_device(): lax.psum_scatter(contract_last(normed, unembed), 'wide', scatter_dimensio...  120 us
    psum x1, waiting for transfers between devices, per_device(): label_grads = lax.psum(label_part, 'narrow')  90 us
    all_to_all x1, blocking collectives, per_device(): lax.all_to_all(label_grads, 'wide', split_axis=0, concat_axis=1, tiled=True)  58.3 us
    all_gather x1, waiting for transfers between devices, per_device(): lax.all_gather(probs, 'wide', axis=0, tiled=True)  34.7 us
    all_to_all x1, blocking collectives, per_device(): lax.all_to_all(resid, 'wide', split_axis=1, concat_axis=0, tiled=True)  26.2 us
  transfers between devices with their start and end apart: 6, of which 5 were waited for; matrix products, arithmetic and copies ran while one was open for 5% of the time, Pallas kernels for 0%

profile of v1, /device:TPU:70, one launch (start us, length us, event | category | flops | bytes accessed | tf_op | source)
XLA Modules:
  0.0 1288.3 jit_solution(7564494500762712051)
XLA Ops:
  8.6 26.2 %all_to_all.71 = bf16[32,32,160]{2,0,1:T(8,128)(2,1)S(1)} all-to-all(bf16[32,32,160]{2,0,1:T(8,128)(2,1)S(1)} %copy.55), channel_id=1, replica_groups=mesh['wide'=32,'narrow'=8] {'wide'}, dimensions={1} | all-to-all | bytes 655360 | tf_op jit(solution)/shard_map/all_to_all | solution.py:44
  35.8 6.7 all-to-all-start.1
  43.3 6.0 all-to-all-done.1
  49.6 4.5 fusion.10
  54.1 119.8 %reduce-scatter.2.cloned.1.call-done = f32[32,2048]{1,0:T(8,128)} async-done(((f32[1024,2048]{1,0:T(8,128)}), f32[32,2048]{1,0:T(8,128)}) %reduce-scatter.2.cloned.1.call-update) | async-done | bytes 262160 | tf_op jit(solution)/shard_map/reduce_scatter | solution.py:52
  175.0 10.2 all_to_all.72
  186.4 8.5 all_to_all.73
  202.6 16.9 %gather_fusion = bf16[4096,160]{1,0:T(8,128)(2,1)} fusion(bf16[2048,160]{1,0:T(8,128)(2,1)S(1)} %copy.62, s32[4096]{0:T(1024)S(1)} %broadcast_clamp_fusion), kind=kCustom, calls=%fused_computation | custom fusion | bytes 2637824 | tf_op jit(solution)/shard_map/jit(_take)/gather | solution.py:67
  219.6 34.7 %all-gather.3.cloned.1.call-done = bf16[1024,2048]{1,0:T(8,128)(2,1)} async-done(((bf16[32,2048]{1,0:T(8,128)(2,1)}), bf16[1024,2048]{1,0:T(8,128)(2,1)}) %all-gather.3.cloned.1.call-update) | async-done | bytes 4194320 | tf_op jit(solution)/shard_map/all_gather | solution.py:60
  260.4 5.3 sub.34
  265.7 7.0 multiply_subtract_fusion
  272.7 5.1 copy.64
  277.8 90.0 %all-reduce.4.cloned.1.call-done = f32[32,128,160]{1,2,0:T(8,128)} async-done(((f32[32,128,160]{1,2,0:T(8,128)}), f32[32,128,160]{1,2,0:T(8,128)}) %all-reduce.4.cloned.1.call-update) | async-done | bytes 2621456 | tf_op jit(solution)/shard_map/psum | solution.py:71
  367.8 58.3 %all_to_all.74 = f32[32,128,160]{1,2,0:T(8,128)} all-to-all(f32[32,128,160]{1,2,0:T(8,128)} %all-reduce.4.cloned.1.call-done), channel_id=1, replica_groups=mesh['wide'=32,'narrow'=8] {'wide'}, dimensions={0} | all-to-all | bytes 5242880 | tf_op jit(solution)/shard_map/all_to_all | solution.py:72
  426.1 6.5 stack.2
  432.6 18.5 %all-to-all-start.5 = ((bf16[32,1728,160]{1,2,0:T(8,128)(2,1)}), bf16[32,1728,160]{1,2,0:T(8,128)(2,1)}, u32[]{:S(2)}, u32[]{:S(2)}) async-start(bf16[32,1728,160]{1,2,0:T(8,128)(2,1)} %stack.2), calls=%async_computation.6 | async-start | bytes 36700160 | tf_op jit(solution)/shard_map/all_to_all | solution.py:85
  453.3 5.6 mul.160
  461.5 5.6 mul.139
  469.4 5.7 mul.155
  475.1 5.1 copy.65
  480.2 4.6 fusion.3
  486.1 4.5 fusion.1
  490.6 4.5 convert_element_type.56
  495.2 357.9 %all-to-all-done.5 = bf16[32,1728,160]{1,2,0:T(8,128)(2,1)} async-done(((bf16[32,1728,160]{1,2,0:T(8,128)(2,1)}), bf16[32,1728,160]{1,2,0:T(8,128)(2,1)}, u32[]{:S(2)}, u32[]{:S(2)}) %all-to-all-start.5) | async-done | bytes 17694752 | tf_op jit(solution)/shard_map/all_to_all | solution.py:85
  853.0 9.1 fusion.5
  864.5 18.9 %all_to_all.75 = bf16[32,32,160]{2,0,1:T(8,128)(2,1)S(1)} all-to-all(bf16[32,32,160]{2,0,1:T(8,128)(2,1)S(1)} %copy.70), channel_id=1, replica_groups=mesh['wide'=32,'narrow'=8] {'wide'}, dimensions={1} | all-to-all | bytes 655360 | tf_op jit(solution)/shard_map/all_to_all | solution.py:45
  885.4 210.0 %all-reduce.6 = bf16[1024,640]{1,0:T(8,128)(2,1)S(1)} all-reduce(f32[1024,640]{1,0:T(8,128)} %fusion.13), channel_id=1, replica_groups=mesh['wide'=32,'narrow'=8] {'wide'}, use_global_device_ids=true, to_apply=%region_11.12 | all-reduce | flops 655360 | bytes 3932160 | tf_op jit(solution)/shard_map/psum | solution.py:99
  1095.4 11.7 fusion.12
  1107.1 154.5 %all-reduce.5 = bf16[4096,432]{0,1:T(8,128)(2,1)} all-reduce(f32[4096,432]{0,1:T(8,128)} %fusion.12), channel_id=1, replica_groups=mesh['wide'=32,'narrow'=8] {'narrow'}, use_global_device_ids=true, to_apply=%region_10.11 | all-reduce | flops 1769472 | bytes 10616832 | tf_op jit(solution)/shard_map/psum | solution.py:97
  1261.6 6.4 copy.69
  1268.0 7.0 reshape.141
  1275.0 5.6 multiply_reduce_fusion
  (73 shorter events, 34.1 us)
Async XLA Ops:
  6.5 1088.9 %copy-start = (bf16[1728,432]{0,1:T(8,128)(2,1)S(1)}, bf16[1728,432]{0,1:T(8,128)(2,1)}, u32[]{:S(2)}) copy-start(bf16[1728,432]{0,1:T(8,128)(2,1)} %param.17) | copy-start | bytes 4478980
  6.5 43.0 %copy-start.4 = (bf16[2048,160]{0,1:T(8,128)(2,1)S(1)}, bf16[2048,160]{0,1:T(8,128)(2,1)}, u32[]{:S(2)}) copy-start(bf16[2048,160]{0,1:T(8,128)(2,1)} %param.11) | copy-start | bytes 1966084
  35.8 13.5 %all-to-all-start.1 = ((f32[32,1,1024]{2,1,0:T(1,128)}), f32[32,1,1024]{2,1,0:T(1,128)S(1)}, u32[]{:S(2)}, u32[]{:S(2)}) async-start(f32[32,1,1024]{2,1,0:T(1,128)} %broadcast_in_dim.40), calls=%async_computation.1 | async-start | bytes 262144 | tf_op jit(solution)/shard_map/all_to_all | solution.py:14
  42.5 131.5 %reduce-scatter.2.cloned.1.call-start = ((), (), s32[]{:S(2)}) async-start(), calls=%async_computation.8 | async-start | bytes 8650752 | tf_op jit(solution)/shard_map/reduce_scatter | solution.py:52
  54.1 143.2 %copy-start.10 = (s32[1024,4]{0,1:T(4,128)S(1)}, s32[1024,4]{0,1:T(4,128)}, u32[]{:S(2)}) copy-start(s32[1024,4]{0,1:T(4,128)} %param.12) | copy-start | bytes 49156
  54.1 200.2 %all-gather.3.cloned.1.call-start = ((), (), s32[]{:S(2)}) async-start(), calls=%async_computation.9 | async-start | bytes 4325376 | tf_op jit(solution)/shard_map/all_gather | solution.py:60
  196.7 171.1 %all-reduce.4.cloned.1.call-start = ((), (), s32[]{:S(2)}) async-start(), calls=%async_computation.10 | async-start | bytes 5242880 | tf_op jit(solution)/shard_map/psum | solution.py:71
  277.8 148.3 %copy-start.5 = (bf16[1728,160]{0,1:T(8,128)(2,1)S(1)}, bf16[1728,160]{0,1:T(8,128)(2,1)}, u32[]{:S(2)}) copy-start(bf16[1728,160]{0,1:T(8,128)(2,1)} %param.15) | copy-start | bytes 1658884
  432.6 18.5 %copy-start.9 = (f32[5120]{0:T(1024)S(1)}, f32[5120]{0:T(1024)}, u32[]{:S(2)}) copy-start(f32[5120]{0:T(1024)} %param.10) | copy-start | bytes 61444
  432.6 18.6 %copy-start.3 = (bf16[32,5120]{1,0:T(8,128)(2,1)S(1)}, bf16[32,5120]{1,0:T(8,128)(2,1)}, u32[]{:S(2)}) copy-start(bf16[32,5120]{1,0:T(8,128)(2,1)} %param.9) | copy-start | bytes 983044
  432.6 420.5 %all-to-all-start.5 = ((bf16[32,1728,160]{1,2,0:T(8,128)(2,1)}), bf16[32,1728,160]{1,2,0:T(8,128)(2,1)}, u32[]{:S(2)}, u32[]{:S(2)}) async-start(bf16[32,1728,160]{1,2,0:T(8,128)(2,1)} %stack.2), calls=%async_computation.6 | async-start | bytes 36700160 | tf_op jit(solution)/shard_map/all_to_all | solution.py:85
  451.1 644.3 %all-gather.5.cloned.1.call-start = ((), (), s32[]{:S(2)}) async-start(), calls=%async_computation.11 | async-start | bytes 15138816 | tf_op jit(solution)/shard_map/all_gather | solution.py:93
  469.4 5.7 copy-start.8
  480.2 4.7 copy-start.1
  480.2 5.9 copy-start.2
  853.0 10.5 copy-start.6
  862.1 21.2 %copy-start.7 = (bf16[160,640]{1,0:T(8,128)(2,1)S(1)}, bf16[160,640]{1,0:T(8,128)(2,1)}, u32[]{:S(2)}) copy-start(bf16[160,640]{1,0:T(8,128)(2,1)} %param.16) | copy-start | bytes 614404
Sparse Core Ops, SparseCore 0:
  54.2 119.6 reduce-scatter.1
  196.8 57.4 all-gather.2
  277.9 89.8 all-reduce.3
  863.6 138.0 all-gather.4
